TPU v7x, 32 devices: a whole 2x2x4 slice. The times are simulated.
32 devices in a mesh: lat: 8 (over z, y), lon: 4 (over x, core).
Axes of the slice: x: 2, y: 2, z: 4, core: 2. Of those that a mesh axis runs over, the one named last changes fastest.
Arguments:
- grid_field: float32 [384, 64, 512], P(None, 'lat', 'lon'), may hold values from -6 to 6
- disco_dlat: int32 [64, 16], P('lat'), may hold values from -2 to 2
- disco_dlon: int32 [64, 16], P('lat'), may hold values from -2 to 2
- disco_basis: int32 [64, 16], P('lat'), may hold values from 0 to 3
- disco_quad: float32 [64, 16], P('lat'), may hold values from 0.05 to 0.5
- disco_weight: bfloat16 [4, 384, 384], replicated, may hold values from -0.3125 to 0.3125
- norm_gain: float32 [384], replicated, may hold values from 0.1 to 1.9
- spectral_filter: float32 [384, 64], replicated, may hold values from -6 to 6
- mix_weight: bfloat16 [384, 384], replicated, may hold values from -0.3125 to 0.3125
Outputs:
- updated: float32 [384, 64, 512], P(None, 'lat', 'lon')
All inputs are finite; a program needn't handle non-finite values.
Results may differ from a plain program's by a relative error of at most 0.0044.
Values may be sent and summed in bfloat16 or wider, within the bound.
A program may use at most 64 MiB of HBM per device.

v0:
```python
import math
import jax
import jax.numpy as jnp
from jax import lax
from jax.sharding import PartitionSpec as P

M_DEV = 8
HALO = 2


def padded_2(cells, sides, width):
    for axis, dim in sides:
        count = lax.axis_size(axis)
        head = lax.slice_in_dim(cells, 0, width, axis=dim)
        tail = lax.slice_in_dim(cells, cells.shape[dim] - width, cells.shape[dim], axis=dim)
        cells = jnp.concatenate(
            [
                lax.ppermute(tail, axis, [(i, (i + 1) % count) for i in range(count)]),
                cells,
                lax.ppermute(head, axis, [((i + 1) % count, i) for i in range(count)]),
            ],
            axis=dim,
        )
    return cells


def legendre_table(first_order, local_orders, all_orders, degrees, nlat):
    lat_pos = jnp.arange(nlat, dtype=jnp.float32)
    colatitude = math.pi * (lat_pos + 0.5) / nlat
    cosine = jnp.cos(colatitude)
    sine = jnp.sin(colatitude)
    counters = jnp.arange(1, all_orders, dtype=jnp.float32)
    cumulative = jnp.concatenate(
        [
            jnp.zeros((1,), jnp.float32),
            jnp.cumsum(jnp.log((2.0 * counters - 1.0) / (2.0 * counters))),
        ]
    )
    log_product = lax.dynamic_slice_in_dim(cumulative, first_order, local_orders)
    orders = first_order + jnp.arange(local_orders, dtype=jnp.int32)
    order_real = orders.astype(jnp.float32)[:, None]
    log_seed = (
        0.5 * (jnp.log((2.0 * order_real + 1.0) / (4.0 * math.pi)) + log_product[:, None])
        + order_real * jnp.log(sine)[None, :]
    )
    rescale = jnp.clip(-log_seed, 0.0, 80.0)
    seed_value = jnp.exp(log_seed + rescale)
    undo = jnp.exp(-rescale)

    def advance(state_pair, degree):
        previous, before_last = state_pair
        degree_real = degree.astype(jnp.float32)
        factor_a = jnp.sqrt(
            jnp.maximum(4.0 * degree_real**2 - 1.0, 1.0)
            / jnp.maximum(degree_real**2 - order_real**2, 1.0)
        )
        factor_b = jnp.sqrt(
            jnp.maximum((degree_real - 1.0) ** 2 - order_real**2, 0.0)
            / jnp.maximum(4.0 * (degree_real - 1.0) ** 2 - 1.0, 1.0)
        )
        recurred = factor_a * (cosine[None, :] * previous - factor_b * before_last)
        current = jnp.where(
            degree == orders[:, None],
            seed_value,
            jnp.where(degree > orders[:, None], recurred, 0.0),
        )
        return ((current, previous), current * undo)

    empty = jnp.zeros((local_orders, nlat), jnp.float32)
    final_pair, table = lax.scan(
        advance, (empty, empty), jnp.arange(degrees, dtype=jnp.int32), unroll=8
    )
    return table


def disco_rows(padded, disco_dlat, disco_dlon, disco_basis, disco_quad, disco_weight, width):
    basis_count = disco_weight.shape[0]
    channels = padded.shape[0]
    zero_index = jnp.zeros((), jnp.int32)

    def one_row(inputs):
        row_index, lat_offsets, lon_offsets, basis_row, quad_row = inputs
        sources = row_index + HALO + lat_offsets
        begins = HALO + lon_offsets

        def take(source, begin):
            return lax.dynamic_slice(padded, (zero_index, source, begin), (channels, 1, width))[
                :, 0, :
            ]

        support = jax.vmap(take)(sources, begins)
        selector = (basis_row[:, None] == jnp.arange(basis_count, dtype=jnp.int32)[None, :]).astype(
            jnp.float32
        ) * quad_row[:, None]
        aggregate = jnp.einsum(
            "kb,kcj->bcj", selector, support, precision=lax.Precision.HIGHEST
        ).astype(jnp.bfloat16)
        return lax.dot_general(
            disco_weight,
            aggregate,
            (((0, 1), (0, 1)), ((), ())),
            preferred_element_type=jnp.float32,
        )

    row_count = disco_dlat.shape[0]
    stacked = lax.map(
        one_row,
        (jnp.arange(row_count, dtype=jnp.int32), disco_dlat, disco_dlon, disco_basis, disco_quad),
    )
    return jnp.transpose(stacked, (1, 0, 2))


def per_device(
    grid_field,
    disco_dlat,
    disco_dlon,
    disco_basis,
    disco_quad,
    disco_weight,
    norm_gain,
    spectral_filter,
    mix_weight,
):
    lat_count = lax.axis_size("lat")
    lon_count = lax.axis_size("lon")
    channels, lat_local, lon_local = grid_field.shape
    lat_total = lat_local * lat_count
    lon_total = lon_local * lon_count
    mode_count = M_DEV * lat_count
    chan_local = channels // lon_count
    lat_index = lax.axis_index("lat")
    lon_index = lax.axis_index("lon")
    wrapped = padded_2(grid_field, (("lat", 1), ("lon", 2)), HALO)
    global_rows = lat_index * lat_local + jnp.arange(lat_local + 2 * HALO, dtype=jnp.int32) - HALO
    inside = (global_rows >= 0) & (global_rows < lat_total)
    padded = jnp.where(inside[None, :, None], wrapped, 0.0)
    after_conv = grid_field + disco_rows(
        padded, disco_dlat, disco_dlon, disco_basis, disco_quad, disco_weight, lon_local
    )
    mean_square = jnp.mean(after_conv * after_conv, axis=0, keepdims=True)
    normed = after_conv * lax.rsqrt(mean_square + 1e-06) * norm_gain[:, None, None]
    lon_pos = jnp.arange(lon_total, dtype=jnp.int32)
    mode_pos = jnp.arange(mode_count, dtype=jnp.int32)
    phase = (lon_pos[:, None] * mode_pos[None, :] % lon_total).astype(jnp.float32) * (
        2.0 * math.pi / lon_total
    )
    cos_part = jnp.cos(phase)
    sin_part = jnp.sin(phase)
    forward_table = jnp.concatenate([cos_part, -sin_part], axis=1) * (2.0 * math.pi / lon_total)
    mode_weight = jnp.where(mode_pos == 0, 1.0, 2.0).astype(jnp.float32)[None, :]
    inverse_table = jnp.transpose(
        jnp.concatenate([cos_part * mode_weight, -sin_part * mode_weight], axis=1)
    )
    portion = lax.all_to_all(normed, "lon", split_axis=0, concat_axis=2, tiled=True)
    result = jnp.einsum("crj,jq->qcr", portion, forward_table, precision=lax.Precision.HIGHEST)
    fourier = result.reshape(2, mode_count, portion.shape[0], portion.shape[1])
    table = legendre_table(lat_index * M_DEV, M_DEV, mode_count, mode_count, lat_total)
    lat_pos = jnp.arange(lat_total, dtype=jnp.float32)
    quad_weight = math.pi / lat_total * jnp.sin(math.pi * (lat_pos + 0.5) / lat_total)
    local_filter = lax.dynamic_slice_in_dim(spectral_filter, lon_index * chan_local, chan_local, 0)
    weighted = lax.all_to_all(fourier, "lat", split_axis=1, concat_axis=3, tiled=True) * quad_weight
    spectra = jnp.einsum("rmck,lmk->rmcl", weighted, table, precision=lax.Precision.HIGHEST)
    filtered = spectra * local_filter[None, None]
    synthesis = jnp.einsum("rmcl,lmk->rmck", filtered, table, precision=lax.Precision.HIGHEST)
    returned = lax.all_to_all(synthesis, "lat", split_axis=3, concat_axis=1, tiled=True)
    wave_field = jnp.einsum(
        "qcr,qj->crj",
        returned.reshape(2 * mode_count, chan_local, lat_local),
        inverse_table,
        precision=lax.Precision.HIGHEST,
    )
    activated_local = jax.nn.gelu(wave_field, approximate=True).astype(jnp.bfloat16)
    activated = lax.all_to_all(activated_local, "lon", split_axis=2, concat_axis=0, tiled=True)
    mixed = lax.dot_general(
        mix_weight, activated, (((0,), (0,)), ((), ())), preferred_element_type=jnp.float32
    )
    return after_conv + mixed


def solution(mesh):
    placed = (
        P(None, "lat", "lon"),
        P("lat", None),
        P("lat", None),
        P("lat", None),
        P("lat", None),
        P(),
        P(),
        P(),
        P(),
    )
    return jax.shard_map(
        per_device, mesh=mesh, in_specs=placed, out_specs=P(None, "lat", "lon"), check_vma=False
    )
```

profile of v0, /device:TPU:0, one launch (start us, length us, event | category | flops | bytes accessed | tf_op | source)
XLA Modules:
  0.0 368.7 jit_solution(16414946515964665758)
XLA Ops:
  9.4 14.1 %collective-permute-done = f32[384,2,128]{0,1,2:T(2,128)} collective-permute-done((f32[384,2,128]{0,1,2:T(2,128)}, f32[384,2,128]{0,1,2:T(2,128)}, u32[]{:S(2)}, u32[]{:S(2)}) %collective-permute-start) | collective-permute-done | bytes 393248 | tf_op jit(solution)/shard_map/ppermute | solution.py:18
  32.9 146.3 %while.33 = (s32[]{:T(128)}, f32[8,384,128]{1,2,0:T(8,128)}, s32[8,16]{1,0:T(8,128)}, f32[8,16]{1,0:T(8,128)}, s32[8]{0:T(128)S(1)}, /*index=5*/s32[8,16]{1,0:T(...) while((s32[]{:T(128)}, f32[8,384,128]{1,2,0:T(8,128)}, ...), condition=%wide.region_1.2_spmd, body=%wide.region_0.1_spmd.sunk | while | flops 188940624 | bytes 22611376 | solution.py:106
  35.0 6.6 %gather_fusion = f32[16,384,128]{1,0,2:T(8,128)} fusion(f32[384,12,132]{0,1,2:T(8,128)S(1)} %get-tuple-element.853, s32[16]{0:T(128)S(1)} %or_bitcast_fusion.2), kind=kCustom, calls=%fused_computation.clone.1 | custom fusion | bytes 6291648 | tf_op jit(solution)/shard_map/while/body/eval_jaxpr/vmap()/gather | solution.py:87
  41.5 3.6 copy.119
  53.3 6.6 %gather_fusion = f32[16,384,128]{1,0,2:T(8,128)} fusion(f32[384,12,132]{0,1,2:T(8,128)S(1)} %get-tuple-element.853, s32[16]{0:T(128)S(1)} %or_bitcast_fusion.2), kind=kCustom, calls=%fused_computation.clone.1 | custom fusion | bytes 6291648 | tf_op jit(solution)/shard_map/while/body/eval_jaxpr/vmap()/gather | solution.py:87
  59.8 3.6 copy.119
  71.6 6.6 %gather_fusion = f32[16,384,128]{1,0,2:T(8,128)} fusion(f32[384,12,132]{0,1,2:T(8,128)S(1)} %get-tuple-element.853, s32[16]{0:T(128)S(1)} %or_bitcast_fusion.2), kind=kCustom, calls=%fused_computation.clone.1 | custom fusion | bytes 6291648 | tf_op jit(solution)/shard_map/while/body/eval_jaxpr/vmap()/gather | solution.py:87
  78.1 3.6 copy.119
  89.8 6.6 %gather_fusion = f32[16,384,128]{1,0,2:T(8,128)} fusion(f32[384,12,132]{0,1,2:T(8,128)S(1)} %get-tuple-element.853, s32[16]{0:T(128)S(1)} %or_bitcast_fusion.2), kind=kCustom, calls=%fused_computation.clone.1 | custom fusion | bytes 6291648 | tf_op jit(solution)/shard_map/while/body/eval_jaxpr/vmap()/gather | solution.py:87
  96.4 3.6 copy.119
  108.1 6.6 %gather_fusion = f32[16,384,128]{1,0,2:T(8,128)} fusion(f32[384,12,132]{0,1,2:T(8,128)S(1)} %get-tuple-element.853, s32[16]{0:T(128)S(1)} %or_bitcast_fusion.2), kind=kCustom, calls=%fused_computation.clone.1 | custom fusion | bytes 6291648 | tf_op jit(solution)/shard_map/while/body/eval_jaxpr/vmap()/gather | solution.py:87
  126.4 6.6 %gather_fusion = f32[16,384,128]{1,0,2:T(8,128)} fusion(f32[384,12,132]{0,1,2:T(8,128)S(1)} %get-tuple-element.853, s32[16]{0:T(128)S(1)} %or_bitcast_fusion.2), kind=kCustom, calls=%fused_computation.clone.1 | custom fusion | bytes 6291648 | tf_op jit(solution)/shard_map/while/body/eval_jaxpr/vmap()/gather | solution.py:87
  132.9 3.6 copy.119
  144.7 6.6 %gather_fusion = f32[16,384,128]{1,0,2:T(8,128)} fusion(f32[384,12,132]{0,1,2:T(8,128)S(1)} %get-tuple-element.853, s32[16]{0:T(128)S(1)} %or_bitcast_fusion.2), kind=kCustom, calls=%fused_computation.clone.1 | custom fusion | bytes 6291648 | tf_op jit(solution)/shard_map/while/body/eval_jaxpr/vmap()/gather | solution.py:87
  151.2 3.6 copy.119
  162.9 6.6 %gather_fusion = f32[16,384,128]{1,0,2:T(8,128)} fusion(f32[384,12,132]{0,1,2:T(8,128)S(1)} %get-tuple-element.853, s32[16]{0:T(128)S(1)} %or_bitcast_fusion.2), kind=kCustom, calls=%fused_computation.clone.1 | custom fusion | bytes 6291648 | tf_op jit(solution)/shard_map/while/body/eval_jaxpr/vmap()/gather | solution.py:87
  169.5 3.6 copy.119
  184.9 3.7 %all-to-all-start = ((f32[384,8,128]{2,1,0:T(8,128)}), f32[384,8,128]{2,1,0:T(8,128)S(1)}, u32[]{:S(2)}, u32[]{:S(2)}) async-start(f32[384,8,128]{2,1,0:T(8,128)} %copy.83), calls=%async_computation | async-start | bytes 3145728 | tf_op jit(solution)/shard_map/all_to_all | solution.py:154
  192.8 15.7 %all-to-all-done = f32[384,8,128]{2,1,0:T(8,128)S(1)} async-done(((f32[384,8,128]{2,1,0:T(8,128)}), f32[384,8,128]{2,1,0:T(8,128)S(1)}, u32[]{:S(2)}, u32[]{:S(2)}) %all-to-all-start) | async-done | bytes 1572896 | tf_op jit(solution)/shard_map/all_to_all | solution.py:154
  216.6 4.6 %all-to-all-start.1 = ((f32[2,64,96,8]{2,3,0,1:T(8,128)}), f32[2,64,96,8]{2,3,0,1:T(8,128)S(1)}, u32[]{:S(2)}, u32[]{:S(2)}) async-start(f32[2,64,96,8]{2,3,0,1:T(8,128)} %copy.85), calls=%async_computation.1 | async-start | bytes 1048576 | tf_op jit(solution)/shard_map/all_to_all | solution.py:161
  221.3 95.3 %while.34 = (s32[]{:T(128)}, f32[8,64]{1,0:T(8,128)S(1)}, f32[8,64]{1,0:T(8,128)S(1)}, f32[8,8,8,64]{3,2,1,0:T(8,128)S(1)}, s32[8,8]{1,0:T(8,128)S(1)}, /*index=...) while((s32[]{:T(128)}, f32[8,64]{1,0:T(8,128)S(1)}, ...), condition=%wide.region_4.5_spmd.clone.clone.clone.clone, body=%wide.region_3.4_spmd.clone.clone.clone.clone.sunk | while | flops 93138 | bytes 238507 | solution.py:70
  320.2 6.0 %all-to-all-start.2 = ((f32[2,8,96,64]{2,0,1,3:T(2,128)}), f32[2,8,96,64]{2,0,1,3:T(2,128)S(1)}, u32[]{:S(2)}, u32[]{:S(2)}) async-start(f32[2,8,96,64]{2,0,1,3:T(2,128)} %copy.91), calls=%async_computation.2 | async-start | bytes 1048576 | tf_op jit(solution)/shard_map/all_to_all | solution.py:165
  327.3 12.6 %all-to-all-done.2 = f32[2,8,96,64]{2,0,1,3:T(2,128)S(1)} async-done(((f32[2,8,96,64]{2,0,1,3:T(2,128)}), f32[2,8,96,64]{2,0,1,3:T(2,128)S(1)}, u32[]{:S(2)}, u32[]{:S(2)}) %all-to-all-start.2) | async-done | bytes 393248 | tf_op jit(solution)/shard_map/all_to_all | solution.py:165
  345.2 17.6 %all_to_all.69 = bf16[96,8,512]{0,1,2:T(8,128)(2,1)} all-to-all(bf16[96,8,512]{0,1,2:T(8,128)(2,1)S(1)} %copy.94), channel_id=1, replica_groups=mesh['lat'=8,'lon'=4] {'lon'}, dimensions={2} | all-to-all | bytes 1572864 | tf_op jit(solution)/shard_map/all_to_all | solution.py:173
  (357 shorter events, 168.8 us)
Async XLA Ops:
  0.0 365.0 %copy-start = (bf16[384,384]{1,0:T(8,128)(2,1)S(1)}, bf16[384,384]{1,0:T(8,128)(2,1)}, u32[]{:S(2)}) copy-start(bf16[384,384]{1,0:T(8,128)(2,1)} %param.21) | copy-start | bytes 884740
  2.0 24.4 %copy-start.3 = (f32[384,8,128]{0,1,2:T(8,128)}, f32[384,8,128]{0,1,2:T(8,128)S(1)}, u32[]{:S(2)}) copy-start(f32[384,8,128]{0,1,2:T(8,128)S(1)} %copy.78) | copy-start | bytes 4718596
  3.3 24.9 %copy-start.4 = (f32[384,8,128]{2,1,0:T(8,128)S(1)}, f32[384,8,128]{2,1,0:T(8,128)}, u32[]{:S(2)}) copy-start(f32[384,8,128]{2,1,0:T(8,128)} %param.13) | copy-start | bytes 4718596
  3.3 20.1 %collective-permute-start = (f32[384,2,128]{0,1,2:T(2,128)}, f32[384,2,128]{0,1,2:T(2,128)}, u32[]{:S(2)}, u32[]{:S(2)}) collective-permute-start(f32[384,2,128]{0,1,2:T(2,128)} %get-tuple-element.570), channel_id=1, source_target_pairs={{0,4},{4,8},{8,12},{12,16},{16,20},{20,24},{24,28},{28,0},{1,5},{5... | collective-permute-start | bytes 1179656 | tf_op jit(solution)/shard_map/ppermute | solution.py:18
  6.3 19.3 %collective-permute-start.1 = (f32[384,2,128]{0,1,2:T(2,128)}, f32[384,2,128]{0,1,2:T(2,128)}, u32[]{:S(2)}, u32[]{:S(2)}) collective-permute-start(f32[384,2,128]{0,1,2:T(2,128)} %get-tuple-element.571), channel_id=1, source_target_pairs={{4,0},{8,4},{12,8},{16,12},{20,16},{24,20},{28,24},{0,28},{5,1},{9... | collective-permute-start | bytes 1179656 | tf_op jit(solution)/shard_map/ppermute | solution.py:20
  26.4 3.6 collective-permute-start.2
  26.5 4.1 %collective-permute-start.3 = (f32[384,12,2]{0,1,2:T(8,128)S(1)}, f32[384,12,2]{0,1,2:T(8,128)}, u32[]{:S(2)}, u32[]{:S(2)}) collective-permute-start(f32[384,12,2]{0,1,2:T(8,128)S(1)} %get-tuple-element.569), channel_id=1, source_target_pairs={{1,0},{2,1},{3,2},{0,3},{5,4},{6,5},{7,6},{4,7},{9,8},{10,9},{11,1... | collective-permute-start | bytes 110600 | tf_op jit(solution)/shard_map/ppermute | solution.py:20
  30.0 0.6 copy-start.6
  46.5 3.6 copy-start.1
  64.8 3.6 copy-start.1
  83.1 3.6 copy-start.1
  101.4 3.6 copy-start.1
  119.7 3.6 copy-start.1
  137.9 3.6 copy-start.1
  156.2 3.6 copy-start.1
  174.5 3.6 copy-start.1
  179.2 2.4 copy-start.2
  179.2 2.4 copy-start.7
  184.9 23.6 %all-to-all-start = ((f32[384,8,128]{2,1,0:T(8,128)}), f32[384,8,128]{2,1,0:T(8,128)S(1)}, u32[]{:S(2)}, u32[]{:S(2)}) async-start(f32[384,8,128]{2,1,0:T(8,128)} %copy.83), calls=%async_computation | async-start | bytes 3145728 | tf_op jit(solution)/shard_map/all_to_all | solution.py:154
  215.5 5.7 %copy-start.5 = (f32[8,8,8,64]{3,2,1,0:T(8,128)S(1)}, f32[8,8,8,64]{3,2,1,0:T(8,128)}, u32[]{:S(2)}) copy-start(f32[8,8,8,64]{3,2,1,0:T(8,128)} %custom-call.6) | copy-start | bytes 393220
  216.6 101.1 %all-to-all-start.1 = ((f32[2,64,96,8]{2,3,0,1:T(8,128)}), f32[2,64,96,8]{2,3,0,1:T(8,128)S(1)}, u32[]{:S(2)}, u32[]{:S(2)}) async-start(f32[2,64,96,8]{2,3,0,1:T(8,128)} %copy.85), calls=%async_computation.1 | async-start | bytes 1048576 | tf_op jit(solution)/shard_map/all_to_all | solution.py:161
  320.2 19.7 %all-to-all-start.2 = ((f32[2,8,96,64]{2,0,1,3:T(2,128)}), f32[2,8,96,64]{2,0,1,3:T(2,128)S(1)}, u32[]{:S(2)}, u32[]{:S(2)}) async-start(f32[2,8,96,64]{2,0,1,3:T(2,128)} %copy.91), calls=%async_computation.2 | async-start | bytes 1048576 | tf_op jit(solution)/shard_map/all_to_all | solution.py:165
where the time goes:
time: 371 us; the launch traced here: 369 us
  local copies, waits for them, and re-layouts  126 us (34%)
  other arithmetic  63.9 us (17%)
  loops' own time  47.8 us (13%)
  matrix products  46.6 us (13%)
  waiting for transfers between devices  44.6 us (12%)
  starting transfers between devices  22.2 us (6%)
  blocking collectives  17.6 us (5%)
    gather x16, local copies, waits for them, and re-layouts, take(): lax.dynamic_slice(padded, (zero_index, source, begin), (channels, 1, width))  81.2 us
    another operation x1, loops' own time, legendre_table(): lax.scan(advance, (empty, empty), jnp.arange(degrees, dtype=jnp.int32), u...  42.2 us
    gt x64, other arithmetic, advance(): degree > orders[:, None]  40.5 us
    dot_general x8, matrix products, one_row(): jnp.einsum('kb,kcj->bcj', selector, support, precision=lax.Precision.HIGH...  28.7 us
    all_to_all x1, blocking collectives, per_device(): lax.all_to_all(activated_local, 'lon', split_axis=2, concat_axis=0, tiled...  17.6 us
    all_to_all x1, waiting for transfers between devices, per_device(): lax.all_to_all(normed, 'lon', split_axis=0, concat_axis=2, tiled=True)  15.7 us
    ppermute x2, waiting for transfers between devices, padded_2(): lax.ppermute(tail, axis, [(i, (i + 1) % count) for i in range(count)])  14.1 us
    all_to_all x1, waiting for transfers between devices, per_device(): lax.all_to_all(synthesis, 'lat', split_axis=3, concat_axis=1, tiled=True)  12.6 us
  transfers between devices with their start and end apart: 7, of which 5 were waited for; matrix products, arithmetic and copies ran while one was open for 17% of the time, Pallas kernels for 0%

commit v1 on v0

--- a/solution.py
+++ b/solution.py
@@ -6,6 +6,29 @@
 
 M_DEV = 8
 HALO = 2
+
+
+def split_up(shard, dim, length):
+    dims = shard.shape
+    pieces = shard.reshape(*dims[:dim], length, dims[dim] // length, *dims[dim + 1 :])
+    return jnp.moveaxis(pieces, dim, 0)
+
+
+def in_order(blocks, dim):
+    shape = list(blocks.shape[1:])
+    shape[dim] *= blocks.shape[0]
+    return jnp.moveaxis(blocks, 0, dim).reshape(shape)
+
+
+def sent_to_each(x, axis, split_dim, concat_dim):
+    size, position = (lax.axis_size(axis), lax.axis_index(axis))
+    parts = split_up(x, split_dim, size)
+    finished = [parts[position]]
+    for turn in range(1, size):
+        sent = parts[(position + turn) % size]
+        finished.append(lax.ppermute(sent, axis, [(i, (i + turn) % size) for i in range(size)]))
+    parts = jnp.stack(finished)[(position - jnp.arange(size)) % size]
+    return in_order(parts, concat_dim)
 
 
 def padded_2(cells, sides, width):
@@ -170,7 +193,7 @@
         precision=lax.Precision.HIGHEST,
     )
     activated_local = jax.nn.gelu(wave_field, approximate=True).astype(jnp.bfloat16)
-    activated = lax.all_to_all(activated_local, "lon", split_axis=2, concat_axis=0, tiled=True)
+    activated = sent_to_each(activated_local, "lon", 2, 0)
     mixed = lax.dot_general(
         mix_weight, activated, (((0,), (0,)), ((), ())), preferred_element_type=jnp.float32
     )

time: 371 us -> 360 us (0.970)
  blocking collectives: 17.6 us -> 0 us
  waiting for transfers between devices: 44.6 us -> 52 us
    all_to_all x1 -> x0, blocking collectives: 17.6 us -> none  [per_device(): lax.all_to_all(activated_local, 'lon', split_axis=2, concat_axis=0, tiled...]
    ppermute x0 -> x3, waiting for transfers between devices: none -> 7.44 us  [sent_to_each(): lax.ppermute(sent, axis, [(i, (i + turn) % size) for i in range(size)])]
  transfers between devices with their start and end apart: 7 -> 10, of which waited for: 5 -> 8; matrix products, arithmetic and copies ran while one was open for 17% -> 17% of each run, Pallas kernels for 0% -> 0%
where the time goes in v1:
time: 360 us; the launch traced here: 356 us
  local copies, waits for them, and re-layouts  123 us (34%)
  other arithmetic  63.4 us (18%)
  waiting for transfers between devices  52 us (14%)
  loops' own time  46.8 us (13%)
  matrix products  46 us (13%)
  starting transfers between devices  24.6 us (7%)
    gather x16, local copies, waits for them, and re-layouts, take(): lax.dynamic_slice(padded, (zero_index, source, begin), (channels, 1, width))  81.1 us
    another operation x1, loops' own time, legendre_table(): lax.scan(advance, (empty, empty), jnp.arange(degrees, dtype=jnp.int32), u...  41.6 us
    gt x64, other arithmetic, advance(): degree > orders[:, None]  39.9 us
    dot_general x8, matrix products, one_row(): jnp.einsum('kb,kcj->bcj', selector, support, precision=lax.Precision.HIGH...  28.7 us
    all_to_all x1, waiting for transfers between devices, per_device(): lax.all_to_all(normed, 'lon', split_axis=0, concat_axis=2, tiled=True)  15.7 us
    ppermute x2, waiting for transfers between devices, padded_2(): lax.ppermute(tail, axis, [(i, (i + 1) % count) for i in range(count)])  14.1 us
    all_to_all x1, waiting for transfers between devices, per_device(): lax.all_to_all(synthesis, 'lat', split_axis=3, concat_axis=1, tiled=True)  12.6 us
    dot_general x8, matrix products, one_row(): lax.dot_general(disco_weight, aggregate, (((0, 1), (0, 1)), ((), ())), pr...  8.78 us
  transfers between devices with their start and end apart: 10, of which 8 were waited for; matrix products, arithmetic and copies ran while one was open for 17% of the time, Pallas kernels for 0%

profile of v1, /device:TPU:0, one launch (start us, length us, event | category | flops | bytes accessed | tf_op | source)
XLA Modules:
  0.0 356.3 jit_solution(11122057626709813915)
XLA Ops:
  9.4 14.1 %collective-permute-done = f32[384,2,128]{0,1,2:T(2,128)} collective-permute-done((f32[384,2,128]{0,1,2:T(2,128)}, f32[384,2,128]{0,1,2:T(2,128)}, u32[]{:S(2)}, u32[]{:S(2)}) %collective-permute-start) | collective-permute-done | bytes 393248 | tf_op jit(solution)/shard_map/ppermute | solution.py:41
  32.9 145.7 %while.33 = (s32[]{:T(128)}, f32[8,384,128]{1,2,0:T(8,128)}, s32[8,16]{1,0:T(8,128)}, f32[8,16]{1,0:T(8,128)}, s32[8]{0:T(128)S(1)}, /*index=5*/s32[8,16]{1,0:T(...) while((s32[]{:T(128)}, f32[8,384,128]{1,2,0:T(8,128)}, ...), condition=%wide.region_1.2_spmd, body=%wide.region_0.1_spmd.sunk | while | flops 188940624 | bytes 22611376 | solution.py:129
  34.9 6.5 %gather_fusion = f32[16,384,128]{1,0,2:T(8,128)} fusion(f32[384,12,132]{0,1,2:T(8,128)S(1)} %get-tuple-element.857, s32[16]{0:T(128)S(1)} %or_bitcast_fusion.2), kind=kCustom, calls=%fused_computation.clone.1 | custom fusion | bytes 6291648 | tf_op jit(solution)/shard_map/while/body/eval_jaxpr/vmap()/gather | solution.py:110
  41.5 3.6 %copy.90 = f32[16,384,128]{2,0,1:T(8,128)} copy(f32[16,384,128]{1,0,2:T(8,128)} %gather_fusion) | data formatting | bytes 6291456 | tf_op jit(solution)/shard_map/while/body/eval_jaxpr/vmap()/gather | solution.py:110
  53.2 6.5 %gather_fusion = f32[16,384,128]{1,0,2:T(8,128)} fusion(f32[384,12,132]{0,1,2:T(8,128)S(1)} %get-tuple-element.857, s32[16]{0:T(128)S(1)} %or_bitcast_fusion.2), kind=kCustom, calls=%fused_computation.clone.1 | custom fusion | bytes 6291648 | tf_op jit(solution)/shard_map/while/body/eval_jaxpr/vmap()/gather | solution.py:110
  59.7 3.6 %copy.90 = f32[16,384,128]{2,0,1:T(8,128)} copy(f32[16,384,128]{1,0,2:T(8,128)} %gather_fusion) | data formatting | bytes 6291456 | tf_op jit(solution)/shard_map/while/body/eval_jaxpr/vmap()/gather | solution.py:110
  71.4 6.5 %gather_fusion = f32[16,384,128]{1,0,2:T(8,128)} fusion(f32[384,12,132]{0,1,2:T(8,128)S(1)} %get-tuple-element.857, s32[16]{0:T(128)S(1)} %or_bitcast_fusion.2), kind=kCustom, calls=%fused_computation.clone.1 | custom fusion | bytes 6291648 | tf_op jit(solution)/shard_map/while/body/eval_jaxpr/vmap()/gather | solution.py:110
  77.9 3.6 %copy.90 = f32[16,384,128]{2,0,1:T(8,128)} copy(f32[16,384,128]{1,0,2:T(8,128)} %gather_fusion) | data formatting | bytes 6291456 | tf_op jit(solution)/shard_map/while/body/eval_jaxpr/vmap()/gather | solution.py:110
  89.6 6.5 %gather_fusion = f32[16,384,128]{1,0,2:T(8,128)} fusion(f32[384,12,132]{0,1,2:T(8,128)S(1)} %get-tuple-element.857, s32[16]{0:T(128)S(1)} %or_bitcast_fusion.2), kind=kCustom, calls=%fused_computation.clone.1 | custom fusion | bytes 6291648 | tf_op jit(solution)/shard_map/while/body/eval_jaxpr/vmap()/gather | solution.py:110
  96.1 3.6 %copy.90 = f32[16,384,128]{2,0,1:T(8,128)} copy(f32[16,384,128]{1,0,2:T(8,128)} %gather_fusion) | data formatting | bytes 6291456 | tf_op jit(solution)/shard_map/while/body/eval_jaxpr/vmap()/gather | solution.py:110
  107.8 6.5 %gather_fusion = f32[16,384,128]{1,0,2:T(8,128)} fusion(f32[384,12,132]{0,1,2:T(8,128)S(1)} %get-tuple-element.857, s32[16]{0:T(128)S(1)} %or_bitcast_fusion.2), kind=kCustom, calls=%fused_computation.clone.1 | custom fusion | bytes 6291648 | tf_op jit(solution)/shard_map/while/body/eval_jaxpr/vmap()/gather | solution.py:110
  114.3 3.6 %copy.90 = f32[16,384,128]{2,0,1:T(8,128)} copy(f32[16,384,128]{1,0,2:T(8,128)} %gather_fusion) | data formatting | bytes 6291456 | tf_op jit(solution)/shard_map/while/body/eval_jaxpr/vmap()/gather | solution.py:110
  126.0 6.5 %gather_fusion = f32[16,384,128]{1,0,2:T(8,128)} fusion(f32[384,12,132]{0,1,2:T(8,128)S(1)} %get-tuple-element.857, s32[16]{0:T(128)S(1)} %or_bitcast_fusion.2), kind=kCustom, calls=%fused_computation.clone.1 | custom fusion | bytes 6291648 | tf_op jit(solution)/shard_map/while/body/eval_jaxpr/vmap()/gather | solution.py:110
  132.5 3.6 %copy.90 = f32[16,384,128]{2,0,1:T(8,128)} copy(f32[16,384,128]{1,0,2:T(8,128)} %gather_fusion) | data formatting | bytes 6291456 | tf_op jit(solution)/shard_map/while/body/eval_jaxpr/vmap()/gather | solution.py:110
  144.2 6.5 %gather_fusion = f32[16,384,128]{1,0,2:T(8,128)} fusion(f32[384,12,132]{0,1,2:T(8,128)S(1)} %get-tuple-element.857, s32[16]{0:T(128)S(1)} %or_bitcast_fusion.2), kind=kCustom, calls=%fused_computation.clone.1 | custom fusion | bytes 6291648 | tf_op jit(solution)/shard_map/while/body/eval_jaxpr/vmap()/gather | solution.py:110
  150.7 3.6 %copy.90 = f32[16,384,128]{2,0,1:T(8,128)} copy(f32[16,384,128]{1,0,2:T(8,128)} %gather_fusion) | data formatting | bytes 6291456 | tf_op jit(solution)/shard_map/while/body/eval_jaxpr/vmap()/gather | solution.py:110
  162.4 6.5 %gather_fusion = f32[16,384,128]{1,0,2:T(8,128)} fusion(f32[384,12,132]{0,1,2:T(8,128)S(1)} %get-tuple-element.857, s32[16]{0:T(128)S(1)} %or_bitcast_fusion.2), kind=kCustom, calls=%fused_computation.clone.1 | custom fusion | bytes 6291648 | tf_op jit(solution)/shard_map/while/body/eval_jaxpr/vmap()/gather | solution.py:110
  184.3 3.7 %all-to-all-start = ((f32[384,8,128]{2,1,0:T(8,128)}), f32[384,8,128]{2,1,0:T(8,128)S(1)}, u32[]{:S(2)}, u32[]{:S(2)}) async-start(f32[384,8,128]{2,1,0:T(8,128)} %copy.57), calls=%async_computation | async-start | bytes 3145728 | tf_op jit(solution)/shard_map/all_to_all | solution.py:177
  192.2 15.7 %all-to-all-done = f32[384,8,128]{2,1,0:T(8,128)S(1)} async-done(((f32[384,8,128]{2,1,0:T(8,128)}), f32[384,8,128]{2,1,0:T(8,128)S(1)}, u32[]{:S(2)}, u32[]{:S(2)}) %all-to-all-start) | async-done | bytes 1572896 | tf_op jit(solution)/shard_map/all_to_all | solution.py:177
  216.1 4.6 %all-to-all-start.1 = ((f32[2,64,96,8]{2,3,0,1:T(8,128)}), f32[2,64,96,8]{2,3,0,1:T(8,128)S(1)}, u32[]{:S(2)}, u32[]{:S(2)}) async-start(f32[2,64,96,8]{2,3,0,1:T(8,128)} %copy.59), calls=%async_computation.1 | async-start | bytes 1048576 | tf_op jit(solution)/shard_map/all_to_all | solution.py:184
  220.7 94.3 %while.34 = (s32[]{:T(128)}, f32[8,64]{1,0:T(8,128)S(1)}, f32[8,64]{1,0:T(8,128)S(1)}, f32[8,8,8,64]{3,2,1,0:T(8,128)S(1)}, s32[8,8]{1,0:T(8,128)S(1)}, /*index=...) while((s32[]{:T(128)}, f32[8,64]{1,0:T(8,128)S(1)}, ...), condition=%wide.region_4.5_spmd.clone.clone.clone.clone, body=%wide.region_3.4_spmd.clone.clone.clone.clone.sunk | while | flops 93138 | bytes 238507 | solution.py:93
  318.6 6.0 %all-to-all-start.2 = ((f32[2,8,96,64]{2,0,1,3:T(2,128)}), f32[2,8,96,64]{2,0,1,3:T(2,128)S(1)}, u32[]{:S(2)}, u32[]{:S(2)}) async-start(f32[2,8,96,64]{2,0,1,3:T(2,128)} %copy.65), calls=%async_computation.2 | async-start | bytes 1048576 | tf_op jit(solution)/shard_map/all_to_all | solution.py:188
  325.7 12.6 %all-to-all-done.2 = f32[2,8,96,64]{2,0,1,3:T(2,128)S(1)} async-done(((f32[2,8,96,64]{2,0,1,3:T(2,128)}), f32[2,8,96,64]{2,0,1,3:T(2,128)S(1)}, u32[]{:S(2)}, u32[]{:S(2)}) %all-to-all-start.2) | async-done | bytes 393248 | tf_op jit(solution)/shard_map/all_to_all | solution.py:188
  343.3 4.1 %collective-permute-done.4 = bf16[96,8,128]{2,1,0:T(8,128)(2,1)S(1)} collective-permute-done((bf16[96,8,128]{2,1,0:T(8,128)(2,1)S(1)}, bf16[96,8,128]{2,1,0:T(8,128)(2,1)S(1)}, u32[]{:S(2)}, u32[]{:S(2)}) %collective-permute-start.4) | collective-permute-done | bytes 196640 | tf_op jit(solution)/shard_map/ppermute | solution.py:29
  (364 shorter events, 171.0 us)
Async XLA Ops:
  0.0 352.4 %copy-start = (bf16[384,384]{1,0:T(8,128)(2,1)S(1)}, bf16[384,384]{1,0:T(8,128)(2,1)}, u32[]{:S(2)}) copy-start(bf16[384,384]{1,0:T(8,128)(2,1)} %param.21) | copy-start | bytes 884740
  2.0 24.4 %copy-start.3 = (f32[384,8,128]{0,1,2:T(8,128)}, f32[384,8,128]{0,1,2:T(8,128)S(1)}, u32[]{:S(2)}) copy-start(f32[384,8,128]{0,1,2:T(8,128)S(1)} %copy.52) | copy-start | bytes 4718596
  3.4 24.9 %copy-start.4 = (f32[384,8,128]{2,1,0:T(8,128)S(1)}, f32[384,8,128]{2,1,0:T(8,128)}, u32[]{:S(2)}) copy-start(f32[384,8,128]{2,1,0:T(8,128)} %param.13) | copy-start | bytes 4718596
  3.4 20.1 %collective-permute-start = (f32[384,2,128]{0,1,2:T(2,128)}, f32[384,2,128]{0,1,2:T(2,128)}, u32[]{:S(2)}, u32[]{:S(2)}) collective-permute-start(f32[384,2,128]{0,1,2:T(2,128)} %get-tuple-element.570), channel_id=1, source_target_pairs={{0,4},{4,8},{8,12},{12,16},{16,20},{20,24},{24,28},{28,0},{1,5},{5... | collective-permute-start | bytes 1179656 | tf_op jit(solution)/shard_map/ppermute | solution.py:41
  6.4 19.3 %collective-permute-start.1 = (f32[384,2,128]{0,1,2:T(2,128)}, f32[384,2,128]{0,1,2:T(2,128)}, u32[]{:S(2)}, u32[]{:S(2)}) collective-permute-start(f32[384,2,128]{0,1,2:T(2,128)} %get-tuple-element.571), channel_id=1, source_target_pairs={{4,0},{8,4},{12,8},{16,12},{20,16},{24,20},{28,24},{0,28},{5,1},{9... | collective-permute-start | bytes 1179656 | tf_op jit(solution)/shard_map/ppermute | solution.py:43
  26.5 3.6 %collective-permute-start.2 = (f32[384,12,2]{0,1,2:T(8,128)S(1)}, f32[384,12,2]{0,1,2:T(8,128)S(1)}, u32[]{:S(2)}, u32[]{:S(2)}) collective-permute-start(f32[384,12,2]{0,1,2:T(8,128)S(1)} %get-tuple-element.568), channel_id=1, source_target_pairs={{0,1},{1,2},{2,3},{3,0},{4,5},{5,6},{6,7},{7,4},{8,9},{9,10},{10,1... | collective-permute-start | bytes 110600 | tf_op jit(solution)/shard_map/ppermute | solution.py:41
  26.5 4.1 %collective-permute-start.3 = (f32[384,12,2]{0,1,2:T(8,128)S(1)}, f32[384,12,2]{0,1,2:T(8,128)}, u32[]{:S(2)}, u32[]{:S(2)}) collective-permute-start(f32[384,12,2]{0,1,2:T(8,128)S(1)} %get-tuple-element.569), channel_id=1, source_target_pairs={{1,0},{2,1},{3,2},{0,3},{5,4},{6,5},{7,6},{4,7},{9,8},{10,9},{11,1... | collective-permute-start | bytes 110600 | tf_op jit(solution)/shard_map/ppermute | solution.py:43
  46.5 3.6 %copy-start.1 = (bf16[4,384,384]{2,1,0:T(8,128)(2,1)S(1)}, bf16[4,384,384]{2,1,0:T(8,128)(2,1)}, u32[]{:S(2)}) copy-start(bf16[4,384,384]{2,1,0:T(8,128)(2,1)} %get-tuple-element.858) | copy-start | bytes 3538948 | tf_op jit(solution)/shard_map/while
  64.7 3.6 %copy-start.1 = (bf16[4,384,384]{2,1,0:T(8,128)(2,1)S(1)}, bf16[4,384,384]{2,1,0:T(8,128)(2,1)}, u32[]{:S(2)}) copy-start(bf16[4,384,384]{2,1,0:T(8,128)(2,1)} %get-tuple-element.858) | copy-start | bytes 3538948 | tf_op jit(solution)/shard_map/while
  82.9 3.6 %copy-start.1 = (bf16[4,384,384]{2,1,0:T(8,128)(2,1)S(1)}, bf16[4,384,384]{2,1,0:T(8,128)(2,1)}, u32[]{:S(2)}) copy-start(bf16[4,384,384]{2,1,0:T(8,128)(2,1)} %get-tuple-element.858) | copy-start | bytes 3538948 | tf_op jit(solution)/shard_map/while
  101.1 3.6 %copy-start.1 = (bf16[4,384,384]{2,1,0:T(8,128)(2,1)S(1)}, bf16[4,384,384]{2,1,0:T(8,128)(2,1)}, u32[]{:S(2)}) copy-start(bf16[4,384,384]{2,1,0:T(8,128)(2,1)} %get-tuple-element.858) | copy-start | bytes 3538948 | tf_op jit(solution)/shard_map/while
  119.3 3.6 %copy-start.1 = (bf16[4,384,384]{2,1,0:T(8,128)(2,1)S(1)}, bf16[4,384,384]{2,1,0:T(8,128)(2,1)}, u32[]{:S(2)}) copy-start(bf16[4,384,384]{2,1,0:T(8,128)(2,1)} %get-tuple-element.858) | copy-start | bytes 3538948 | tf_op jit(solution)/shard_map/while
  137.5 3.6 %copy-start.1 = (bf16[4,384,384]{2,1,0:T(8,128)(2,1)S(1)}, bf16[4,384,384]{2,1,0:T(8,128)(2,1)}, u32[]{:S(2)}) copy-start(bf16[4,384,384]{2,1,0:T(8,128)(2,1)} %get-tuple-element.858) | copy-start | bytes 3538948 | tf_op jit(solution)/shard_map/while
  155.7 3.6 %copy-start.1 = (bf16[4,384,384]{2,1,0:T(8,128)(2,1)S(1)}, bf16[4,384,384]{2,1,0:T(8,128)(2,1)}, u32[]{:S(2)}) copy-start(bf16[4,384,384]{2,1,0:T(8,128)(2,1)} %get-tuple-element.858) | copy-start | bytes 3538948 | tf_op jit(solution)/shard_map/while
  173.9 3.6 %copy-start.1 = (bf16[4,384,384]{2,1,0:T(8,128)(2,1)S(1)}, bf16[4,384,384]{2,1,0:T(8,128)(2,1)}, u32[]{:S(2)}) copy-start(bf16[4,384,384]{2,1,0:T(8,128)(2,1)} %get-tuple-element.858) | copy-start | bytes 3538948 | tf_op jit(solution)/shard_map/while
  178.7 2.4 copy-start.2
  178.7 2.4 copy-start.7
  184.3 23.6 %all-to-all-start = ((f32[384,8,128]{2,1,0:T(8,128)}), f32[384,8,128]{2,1,0:T(8,128)S(1)}, u32[]{:S(2)}, u32[]{:S(2)}) async-start(f32[384,8,128]{2,1,0:T(8,128)} %copy.57), calls=%async_computation | async-start | bytes 3145728 | tf_op jit(solution)/shard_map/all_to_all | solution.py:177
  215.0 5.7 %copy-start.5 = (f32[8,8,8,64]{3,2,1,0:T(8,128)S(1)}, f32[8,8,8,64]{3,2,1,0:T(8,128)}, u32[]{:S(2)}) copy-start(f32[8,8,8,64]{3,2,1,0:T(8,128)} %custom-call.8) | copy-start | bytes 393220
  216.1 100.1 %all-to-all-start.1 = ((f32[2,64,96,8]{2,3,0,1:T(8,128)}), f32[2,64,96,8]{2,3,0,1:T(8,128)S(1)}, u32[]{:S(2)}, u32[]{:S(2)}) async-start(f32[2,64,96,8]{2,3,0,1:T(8,128)} %copy.59), calls=%async_computation.1 | async-start | bytes 1048576 | tf_op jit(solution)/shard_map/all_to_all | solution.py:184
  318.6 19.7 %all-to-all-start.2 = ((f32[2,8,96,64]{2,0,1,3:T(2,128)}), f32[2,8,96,64]{2,0,1,3:T(2,128)S(1)}, u32[]{:S(2)}, u32[]{:S(2)}) async-start(f32[2,8,96,64]{2,0,1,3:T(2,128)} %copy.65), calls=%async_computation.2 | async-start | bytes 1048576 | tf_op jit(solution)/shard_map/all_to_all | solution.py:188
  340.8 6.6 %collective-permute-start.4 = (bf16[96,8,128]{2,1,0:T(8,128)(2,1)S(1)}, bf16[96,8,128]{2,1,0:T(8,128)(2,1)S(1)}, u32[]{:S(2)}, u32[]{:S(2)}) collective-permute-start(bf16[96,8,128]{2,1,0:T(8,128)(2,1)S(1)} %get-tuple-element.575), channel_id=1, source_target_pairs={{0,1},{1,2},{2,3},{3,0},{4,5},{5,6},{6,7},{7,4},{8,9},{9,10},{10,1... | collective-permute-start | bytes 589832 | tf_op jit(solution)/shard_map/ppermute | solution.py:29
  340.8 7.8 %collective-permute-start.5 = (bf16[96,8,128]{2,1,0:T(8,128)(2,1)S(1)}, bf16[96,8,128]{2,1,0:T(8,128)(2,1)S(1)}, u32[]{:S(2)}, u32[]{:S(2)}) collective-permute-start(bf16[96,8,128]{2,1,0:T(8,128)(2,1)S(1)} %get-tuple-element.574), channel_id=1, source_target_pairs={{0,2},{1,3},{2,0},{3,1},{4,6},{5,7},{6,4},{7,5},{8,10},{9,11},{10,... | collective-permute-start | bytes 589832 | tf_op jit(solution)/shard_map/ppermute | solution.py:29
  341.9 8.9 %collective-permute-start.6 = (bf16[96,8,128]{2,1,0:T(8,128)(2,1)S(1)}, bf16[96,8,128]{2,1,0:T(8,128)(2,1)S(1)}, u32[]{:S(2)}, u32[]{:S(2)}) collective-permute-start(bf16[96,8,128]{2,1,0:T(8,128)(2,1)S(1)} %get-tuple-element.573), channel_id=1, source_target_pairs={{0,3},{1,0},{2,1},{3,2},{4,7},{5,4},{6,5},{7,6},{8,11},{9,8},{10,9... | collective-permute-start | bytes 589832 | tf_op jit(solution)/shard_map/ppermute | solution.py:29
  (1 other events, 0.6 us)
